TPU v7x, 256 devices: a whole 4x4x8 slice. The times are simulated.
256 devices in a mesh: row: 32 (over z, x_lo, core), col: 8 (over y, x_hi).
Axes of the slice: x: 4 (x_hi: 2, x_lo: 2; x = x_hi * 2 + x_lo), y: 4, z: 8, core: 2. Of those that a mesh axis runs over, the one named last changes fastest.
Arguments:
- first_homolog_embedding: bfloat16 [128, 1024, 32], P(None, ('row', 'col')), may hold values from -12 to 12
- second_homolog_embedding: bfloat16 [128, 1024, 32], P(None, ('row', 'col')), may hold values from -12 to 12
- token_chain_index: int32 [1024], replicated, may hold values from 0 to 7, never falling along the last dimension, each value on 1 to 384 neighbouring positions
- incoming_pair_state: bfloat16 [1024, 1024, 128], P('row', 'col'), may hold values from -6 to 6
- tensor_mixing_matrix: bfloat16 [1024, 128], replicated, may hold values from -0.1875 to 0.1875
- outer_product_bias: float32 [128], replicated, may hold values from -3 to 3
- transition_norm_gain: float32 [128], replicated, may hold values from 0.5 to 1.5
- transition_gate_weight: bfloat16 [128, 512], replicated, may hold values from -0.5 to 0.5
- transition_up_weight: bfloat16 [128, 512], replicated, may hold values from -0.5 to 0.5
- transition_down_weight: bfloat16 [512, 128], replicated, may hold values from -0.25 to 0.25
- distogram_weight: bfloat16 [128, 64], replicated, may hold values from -0.5 to 0.5
- distogram_bias: float32 [64], replicated, may hold values from -3 to 3
Outputs:
- pair_out: bfloat16 [1024, 1024, 128], P('row', 'col')
- logits: float32 [64, 1024, 1024], P(None, 'row', 'col')
Inputs may be any that keep to these rules, and one draw needn't show every extreme that they name: `token_chain_index`: chain numbers never fall along the tokens; each chain has 1 to 384 tokens and one chain has exactly 384.
All inputs are finite; a program needn't handle non-finite values.
Results may differ from a plain program's by a relative error of at most 0.006.
Values may be sent and summed in bfloat16 or wider, within the bound.
No kernel may reach another device: no remote copies, remote signals or barrier semaphores. Data moves between devices by JAX's collectives and lax.ppermute only.
A program may use at most 64 MiB of HBM per device.

v0:
```python
import jax
import jax.numpy as jnp
from jax import lax
from jax.sharding import PartitionSpec as P


def layer_norm(values, transition_norm_gain):
    center = jnp.mean(values, axis=-1, keepdims=True)
    shifted = values - center
    spread = jnp.mean(shifted * shifted, axis=-1, keepdims=True)
    return shifted * lax.rsqrt(spread + 1e-05) * transition_norm_gain


def transition_rows(
    mid_rows,
    transition_norm_gain,
    transition_gate_weight,
    transition_up_weight,
    transition_down_weight,
):
    mid_float = mid_rows.astype(jnp.float32)
    normed = layer_norm(mid_float, transition_norm_gain).astype(jnp.bfloat16)
    gate_pre = jnp.dot(normed, transition_gate_weight, preferred_element_type=jnp.float32)
    up_pre = jnp.dot(normed, transition_up_weight, preferred_element_type=jnp.float32)
    hidden = (jax.nn.silu(gate_pre) * up_pre).astype(jnp.bfloat16)
    result = mid_float + jnp.dot(hidden, transition_down_weight, preferred_element_type=jnp.float32)
    return result.astype(jnp.bfloat16)


def transition_tile(
    mid_tile,
    transition_norm_gain,
    transition_gate_weight,
    transition_up_weight,
    transition_down_weight,
):
    tile_shape = mid_tile.shape
    rows_all = tile_shape[0] * tile_shape[1]
    grid_piece = min(512, rows_all)
    blocks = mid_tile.reshape(rows_all // grid_piece, grid_piece, tile_shape[2])

    def one_block(rows):
        return transition_rows(
            rows,
            transition_norm_gain,
            transition_gate_weight,
            transition_up_weight,
            transition_down_weight,
        )

    return lax.map(one_block, blocks).reshape(tile_shape)


def mirror_tile(pair_tile):
    row_count = lax.axis_size("row")
    col_count = lax.axis_size("col")
    rows_tile, cols_tile, channels = pair_tile.shape
    row_groups = row_count // col_count
    step_two = lax.all_to_all(
        lax.all_to_all(pair_tile, "col", split_axis=0, concat_axis=1, tiled=True),
        "row",
        split_axis=1,
        concat_axis=0,
        tiled=True,
    )
    regrouped = step_two.reshape(col_count, row_groups, rows_tile // col_count, rows_tile, channels)
    step_three = lax.all_to_all(regrouped, "col", split_axis=0, concat_axis=2, tiled=True)
    return step_three.reshape(cols_tile, rows_tile, channels)


def per_device(
    first_homolog_embedding,
    second_homolog_embedding,
    token_chain_index,
    incoming_pair_state,
    tensor_mixing_matrix,
    outer_product_bias,
    transition_norm_gain,
    transition_gate_weight,
    transition_up_weight,
    transition_down_weight,
    distogram_weight,
    distogram_bias,
):
    row_at = lax.axis_index("row")
    col_at = lax.axis_index("col")
    rows_tile, cols_tile, channels = incoming_pair_state.shape
    sequence_total_count = first_homolog_embedding.shape[0]
    alignment_slab_length = sequence_total_count // 2
    projection_width = first_homolog_embedding.shape[2]
    left_sequence_rows = lax.all_gather(first_homolog_embedding, "col", axis=1, tiled=True)
    pieces = []
    for alignment_slab_index in range(2):
        gathered = lax.all_gather(
            second_homolog_embedding[
                alignment_slab_index
                * alignment_slab_length : (alignment_slab_index + 1)
                * alignment_slab_length
            ],
            ("row", "col"),
            axis=1,
            tiled=True,
        )
        pieces.append(lax.dynamic_slice_in_dim(gathered, col_at * cols_tile, cols_tile, 1))
    right_cols = jnp.concatenate(pieces, 0)
    chain_rows = lax.dynamic_slice_in_dim(token_chain_index, row_at * rows_tile, rows_tile, 0)
    chain_cols = lax.dynamic_slice_in_dim(token_chain_index, col_at * cols_tile, cols_tile, 0)
    same_chain = (chain_rows[:, None] == chain_cols[None, :]).astype(jnp.float32)
    block_rows = max(1, min(rows_tile, 512 // cols_tile))
    block_count = rows_tile // block_rows
    paired_right = right_cols[:alignment_slab_length]
    unpaired_right = right_cols[alignment_slab_length:]

    def outer_block(block_index):
        row_start = block_index * block_rows
        left_block = lax.dynamic_slice_in_dim(left_sequence_rows, row_start, block_rows, 1)
        chain_mask = lax.dynamic_slice_in_dim(same_chain, row_start, block_rows, 0)
        paired_sum = jnp.einsum(
            "sic,sjd->ijcd",
            left_block[:alignment_slab_length],
            paired_right,
            preferred_element_type=jnp.float32,
        )

        def unpaired_terms():
            return jnp.einsum(
                "sic,sjd->ijcd",
                left_block[alignment_slab_length:],
                unpaired_right,
                preferred_element_type=jnp.float32,
            )

        def no_terms():
            return jnp.zeros_like(paired_sum)

        unpaired_sum = lax.cond(jnp.any(chain_mask > 0.5), unpaired_terms, no_terms)
        weight = chain_mask[:, :, None, None]
        homolog_mean = (paired_sum + weight * unpaired_sum) / (
            alignment_slab_length * (1.0 + weight)
        )
        raveled_matrix = homolog_mean.astype(jnp.bfloat16).reshape(
            block_rows * cols_tile, projection_width * projection_width
        )
        inputs = lax.dynamic_slice_in_dim(incoming_pair_state, row_start, block_rows, 0).reshape(
            block_rows * cols_tile, channels
        )
        middle = jnp.dot(raveled_matrix, tensor_mixing_matrix, preferred_element_type=jnp.float32)
        middle = middle + outer_product_bias + inputs.astype(jnp.float32)
        return middle.astype(jnp.bfloat16).reshape(block_rows, cols_tile, channels)

    pair_mid = lax.map(outer_block, jnp.arange(block_count, dtype=jnp.int32)).reshape(
        rows_tile, cols_tile, channels
    )
    pair_out = transition_tile(
        pair_mid,
        transition_norm_gain,
        transition_gate_weight,
        transition_up_weight,
        transition_down_weight,
    )
    mirror_out = mirror_tile(pair_out)
    own_bins = jnp.einsum(
        "ije,ek->kij", pair_out, distogram_weight, preferred_element_type=jnp.float32
    ).astype(jnp.bfloat16)
    other_bins = jnp.einsum(
        "jie,ek->kij", mirror_out, distogram_weight, preferred_element_type=jnp.float32
    ).astype(jnp.bfloat16)
    logits = (
        own_bins.astype(jnp.float32)
        + other_bins.astype(jnp.float32)
        + distogram_bias[:, None, None]
    )
    return (pair_out, logits)


def solution(mesh):
    placed = (
        P(None, ("row", "col"), None),
        P(None, ("row", "col"), None),
        P(),
        P("row", "col", None),
        P(),
        P(),
        P(),
        P(),
        P(),
        P(),
        P(),
        P(),
    )
    return jax.shard_map(
        per_device,
        mesh=mesh,
        in_specs=placed,
        out_specs=(P("row", "col", None), P(None, "row", "col")),
        check_vma=False,
    )
```

profile of v0, /device:TPU:2, one launch (start us, length us, event | category | flops | bytes accessed | tf_op | source)
XLA Modules:
  0.0 1669.1 jit_solution(15646083899122393495)
XLA Ops:
  7.2 1.5 fusion.57
  11.1 35.4 %all_gather.9 = bf16[128,32,32]{0,2,1:T(8,128)(2,1)S(1)} all-gather(bf16[128,4,32]{0,2,1:T(8,128)(2,1)} %param.18), channel_id=1, replica_groups=mesh['row'=32,'col'=8] {'col'}, dimensions={1}, use_global_device_ids=true | all-gather | bytes 294912 | tf_op jit(solution)/shard_map/all_gather | solution.py:91
  46.6 686.4 %all-gather.3.cloned.1.call-done = bf16[64,1024,32]{0,2,1:T(8,128)(2,1)} async-done(((bf16[64,4,32]{0,2,1:T(8,128)(2,1)}), bf16[64,1024,32]{0,2,1:T(8,128)(2,1)}) %all-gather.3.cloned.1.call-update) | async-done | bytes 4194320 | tf_op jit(solution)/shard_map/all_gather | solution.py:94
  733.0 1.3 constant_dynamic-slice_fusion.4
  735.4 720.9 %all-gather.5.cloned.1.call-done = bf16[64,1024,32]{0,2,1:T(8,128)(2,1)} async-done(((bf16[64,4,32]{0,2,1:T(8,128)(2,1)}), bf16[64,1024,32]{0,2,1:T(8,128)(2,1)}) %all-gather.5.cloned.1.call-update) | async-done | bytes 4194320 | tf_op jit(solution)/shard_map/all_gather | solution.py:94
  1456.3 1.3 constant_dynamic-slice_fusion.3
  1459.3 72.8 %while.20 = (s32[]{:T(128)}, bf16[8,4,128,128]{3,2,1,0:T(8,128)(2,1)}, s32[8]{0:T(128)}, bf16[128,32,32]{0,2,1:T(8,128)(2,1)S(1)}, bf16[64,128,32]{1,0,2:T(8,128...) while((s32[]{:T(128)}, ...), condition=%wide.region_4.5_spmd, body=%wide.region_0.4_spmd.sunk | while | flops 270796800 | bytes 16014713 | solution.py:151
  1459.3 1.3 dynamic_slice.59
  1532.1 46.6 %while.21 = (s32[]{:T(128)}, bf16[8,512,128]{2,1,0:T(8,128)(2,1)}, bf16[8,512,128]{2,1,0:T(8,128)(2,1)}, f32[128]{0:T(128)}, bf16[128,512]{1,0:T(8,128)(2,1)S(1)...) while((s32[]{:T(128)}, bf16[8,512,128]{2,1,0:T(8,128)(2,1)}, ...), condition=%wide.region_8.9_spmd, body=%wide.region_5.8_spmd.sunk | while | flops 204145152 | bytes 3301981 | solution.py:51
  1534.3 1.3 fusion.88
  1535.5 2.4 fusion.89
  1541.4 2.4 fusion.89
  1545.9 1.3 fusion.88
  1547.2 2.4 fusion.89
  1553.0 2.4 fusion.89
  1558.9 2.4 fusion.89
  1563.4 1.3 fusion.88
  1564.7 2.4 fusion.89
  1570.5 2.4 fusion.89
  1576.4 2.4 fusion.89
  1578.7 20.7 %all_to_all.48 = bf16[32,128,128]{2,1,0:T(8,128)(2,1)S(1)} all-to-all(bf16[32,128,128]{2,1,0:T(8,128)(2,1)} %bitcast.126), channel_id=1, replica_groups=mesh['row'=32,'col'=8] {'col'}, dimensions={0} | all-to-all | bytes 2097152 | tf_op jit(solution)/shard_map/all_to_all | solution.py:60
  1600.3 38.7 %all_to_all.49 = bf16[4,1024,128]{2,0,1:T(4,128)(2,1)S(1)} all-to-all(bf16[4,1024,128]{2,0,1:T(4,128)(2,1)S(1)} %copy.46), channel_id=1, replica_groups=mesh['row'=32,'col'=8] {'row'}, dimensions={1} | all-to-all | bytes 2097152 | tf_op jit(solution)/shard_map/all_to_all | solution.py:59
  1639.3 19.6 %all_to_all.50 = bf16[8,4,4,32,128]{4,3,2,1,0:T(8,128)(2,1)S(1)} all-to-all(bf16[8,4,4,32,128]{4,3,2,1,0:T(8,128)(2,1)S(1)} %bitcast.131), channel_id=1, replica_groups=mesh['row'=32,'col'=8] {'col'}, dimensions={0} | all-to-all | bytes 2097152 | tf_op jit(solution)/shard_map/all_to_all | solution.py:67
  1660.7 1.6 copy.50
  (239 shorter events, 98.3 us)
Async XLA Ops:
  7.2 1652.4 %copy-start = (bf16[128,64]{0,1:T(8,128)(2,1)S(1)}, bf16[128,64]{0,1:T(8,128)(2,1)}, u32[]{:S(2)}) copy-start(bf16[128,64]{0,1:T(8,128)(2,1)} %param.28) | copy-start | bytes 49156
  7.2 725.8 %all-gather.3.cloned.1.call-start = ((), (), s32[]{:S(2)}) async-start(), calls=%async_computation.3 | async-start | bytes 8421376 | tf_op jit(solution)/shard_map/all_gather | solution.py:94
  8.8 1447.5 %all-gather.5.cloned.1.call-start = ((), (), s32[]{:S(2)}) async-start(), calls=%async_computation.4 | async-start | bytes 8421376 | tf_op jit(solution)/shard_map/all_gather | solution.py:94
  1459.3 72.8 %copy-start.2 = (bf16[128,512]{1,0:T(8,128)(2,1)S(1)}, bf16[128,512]{1,0:T(8,128)(2,1)}, u32[]{:S(2)}) copy-start(bf16[128,512]{1,0:T(8,128)(2,1)} %param.25) | copy-start | bytes 393220
  1459.3 4.3 copy-start.4
  1465.4 1.8 copy-start.7
  1465.5 2.9 copy-start.5
  1468.4 4.3 copy-start.4
  1474.5 1.8 copy-start.7
  1474.6 2.9 copy-start.5
  1477.5 4.3 copy-start.4
  1483.6 1.8 copy-start.7
  1483.7 2.9 copy-start.5
  1486.6 4.3 copy-start.4
  1492.7 1.8 copy-start.7
  1492.8 2.9 copy-start.5
  1495.7 4.3 copy-start.4
  1501.8 2.9 copy-start.5
  1504.8 4.3 copy-start.4
  1510.9 2.9 copy-start.5
  1513.9 4.3 copy-start.4
  1520.0 2.9 copy-start.5
  1523.0 4.3 copy-start.4
  1529.1 2.9 copy-start.5
  (22 other events, 28.4 us)
Sparse Core Ops, SparseCore 0:
  9.9 723.0 all-gather.2
  734.8 721.4 all-gather.4
where the time goes:
time: 1670 us
  waiting for transfers between devices  1410 us (84%)
  blocking collectives  114 us (7%)
  local copies, waits for them, and re-layouts  47.7 us (3%)
  matrix products  46.7 us (3%)
  other arithmetic  27.3 us (2%)
    all_gather x2, waiting for transfers between devices, per_device(): lax.all_gather(second_homolog_embedding[alignment_slab_index * alignment_...  1410 us
    all_to_all x1, blocking collectives, mirror_tile(): lax.all_to_all(lax.all_to_all(pair_tile, 'col', split_axis=0, concat_axis...  38.7 us
    all_gather x1, blocking collectives, per_device(): lax.all_gather(first_homolog_embedding, 'col', axis=1, tiled=True)  35.4 us
  transfers between devices with their start and end apart: 2, of which 2 were waited for; matrix products, arithmetic and copies ran while one was open for 0% of the time, Pallas kernels for 0%

commit v1 on v0

--- a/solution.py
+++ b/solution.py
@@ -91,15 +91,23 @@
     left_sequence_rows = lax.all_gather(first_homolog_embedding, "col", axis=1, tiled=True)
     pieces = []
     for alignment_slab_index in range(2):
-        gathered = lax.all_gather(
-            second_homolog_embedding[
-                alignment_slab_index
-                * alignment_slab_length : (alignment_slab_index + 1)
-                * alignment_slab_length
-            ],
-            ("row", "col"),
+        gathered = jnp.concatenate(
+            lax.all_to_all(
+                jnp.stack(
+                    [
+                        second_homolog_embedding[
+                            alignment_slab_index
+                            * alignment_slab_length : (alignment_slab_index + 1)
+                            * alignment_slab_length
+                        ]
+                    ]
+                    * lax.axis_size(("row", "col"))
+                ),
+                ("row", "col"),
+                0,
+                0,
+            ),
             axis=1,
-            tiled=True,
         )
         pieces.append(lax.dynamic_slice_in_dim(gathered, col_at * cols_tile, cols_tile, 1))
     right_cols = jnp.concatenate(pieces, 0)

time: 1670 us -> 446 us (0.27)
  waiting for transfers between devices: 1410 us -> 117 us
  local copies, waits for them, and re-layouts: 47.7 us -> 104 us
  starting transfers between devices: 0.08 us -> 24.5 us
    all_gather x2 -> x0, waiting for transfers between devices: 1410 us -> none  [per_device(): lax.all_gather(second_homolog_embedding[alignment_slab_index * alignment_...]
    all_to_all x0 -> x2, waiting for transfers between devices: none -> 117 us  [per_device(): lax.all_to_all(jnp.stack([second_homolog_embedding[alignment_slab_index *...]
    unnamed x9 -> x25, local copies, waits for them, and re-layouts: 1.79 us -> 68.6 us
    all_to_all x0 -> x2, starting transfers between devices: none -> 24.5 us  [per_device(): lax.all_to_all(jnp.stack([second_homolog_embedding[alignment_slab_index *...]
  transfers between devices with their start and end apart: 2 -> 2, of which waited for: 2 -> 2; matrix products, arithmetic and copies ran while one was open for 0% -> 8% of each run, Pallas kernels for 0% -> 0%
where the time goes in v1:
time: 446 us; the launch traced here: 443 us
  waiting for transfers between devices  117 us (26%)
  blocking collectives  115 us (26%)
  local copies, waits for them, and re-layouts  104 us (23%)
  matrix products  48.7 us (11%)
  starting transfers between devices  24.5 us (5%)
  other arithmetic  22.9 us (5%)
  loops' own time  10.9 us (2%)
    all_to_all x2, waiting for transfers between devices, per_device(): lax.all_to_all(jnp.stack([second_homolog_embedding[alignment_slab_index *...  117 us
    unnamed x25, local copies, waits for them, and re-layouts  68.6 us
    all_gather x1, blocking collectives, per_device(): lax.all_gather(first_homolog_embedding, 'col', axis=1, tiled=True)  40.2 us
    all_to_all x1, blocking collectives, mirror_tile(): lax.all_to_all(lax.all_to_all(pair_tile, 'col', split_axis=0, concat_axis...  33.8 us
    all_to_all x2, starting transfers between devices, per_device(): lax.all_to_all(jnp.stack([second_homolog_embedding[alignment_slab_index *...  24.5 us
    all_to_all x1, blocking collectives, mirror_tile(): lax.all_to_all(pair_tile, 'col', split_axis=0, concat_axis=1, tiled=True)  20.7 us
    all_to_all x1, blocking collectives, mirror_tile(): lax.all_to_all(regrouped, 'col', split_axis=0, concat_axis=2, tiled=True)  19.8 us
    dot_general x8, matrix products, transition_rows(): jnp.dot(hidden, transition_down_weight, preferred_element_type=jnp.float32)  18.2 us
  transfers between devices with their start and end apart: 2, of which 2 were waited for; matrix products, arithmetic and copies ran while one was open for 8% of the time, Pallas kernels for 0%

profile of v1, /device:TPU:2, one launch (start us, length us, event | category | flops | bytes accessed | tf_op | source)
XLA Modules:
  0.0 443.0 jit_solution(4505741472401098194)
XLA Ops:
  1.6 5.3 %broadcast_bitcast_fusion.1 = bf16[256,4,32,64]{3,2,1,0:T(8,128)(2,1)} fusion(bf16[64,4,32]{0,2,1:T(8,128)(2,1)S(1)} %get-tuple-element.190), kind=kLoop, calls=%fused_computation.71 | loop fusion | bytes 4210688
  6.9 14.0 %reshape.76 = bf16[256,2,4096]{2,1,0:T(2,128)(2,1)} reshape(bf16[256,4,32,64]{3,2,1,0:T(8,128)(2,1)} %broadcast_bitcast_fusion.1) | data formatting | bytes 8388608
  20.9 15.7 %all-to-all-start = ((bf16[256,2,4096]{2,1,0:T(2,128)(2,1)}), bf16[256,2,4096]{2,1,0:T(2,128)(2,1)}, u32[]{:S(2)}, u32[]{:S(2)}) async-start(bf16[256,2,4096]{2,1,0:T(2,128)(2,1)} %reshape.76), calls=%async_computation | async-start | bytes 8388608 | tf_op jit(solution)/shard_map/all_to_all | solution.py:95
  36.6 5.3 %broadcast_bitcast_fusion = bf16[256,4,32,64]{3,2,1,0:T(8,128)(2,1)} fusion(bf16[64,4,32]{0,2,1:T(8,128)(2,1)S(1)} %get-tuple-element.189), kind=kLoop, calls=%fused_computation.70 | loop fusion | bytes 4210688
  41.9 14.0 %reshape.78 = bf16[256,2,4096]{2,1,0:T(2,128)(2,1)} reshape(bf16[256,4,32,64]{3,2,1,0:T(8,128)(2,1)} %broadcast_bitcast_fusion) | data formatting | bytes 8388608
  55.9 76.9 %all-to-all-done = bf16[256,2,4096]{2,1,0:T(2,128)(2,1)} async-done(((bf16[256,2,4096]{2,1,0:T(2,128)(2,1)}), bf16[256,2,4096]{2,1,0:T(2,128)(2,1)}, u32[]{:S(2)}, u32[]{:S(2)}) %all-to-all-start) | async-done | bytes 4194336 | tf_op jit(solution)/shard_map/all_to_all | solution.py:95
  132.7 8.8 %all-to-all-start.1 = ((bf16[256,2,4096]{2,1,0:T(2,128)(2,1)}), bf16[256,2,4096]{2,1,0:T(2,128)(2,1)}, u32[]{:S(2)}, u32[]{:S(2)}) async-start(bf16[256,2,4096]{2,1,0:T(2,128)(2,1)} %reshape.78), calls=%async_computation.1 | async-start | bytes 8388608 | tf_op jit(solution)/shard_map/all_to_all | solution.py:95
  143.1 40.2 %all_gather.3 = bf16[128,32,32]{0,2,1:T(8,128)(2,1)S(1)} all-gather(bf16[128,4,32]{0,2,1:T(8,128)(2,1)S(1)} %copy-done.3), channel_id=1, replica_groups=mesh['row'=32,'col'=8] {'col'}, dimensions={1}, use_global_device_ids=true | all-gather | bytes 294912 | tf_op jit(solution)/shard_map/all_gather | solution.py:91
  183.4 14.2 %reshape.77 = bf16[256,4,32,64]{3,2,1,0:T(8,128)(2,1)} reshape(bf16[256,2,4096]{2,1,0:T(2,128)(2,1)} %all-to-all-done) | data formatting | bytes 8388608
  197.7 40.1 %all-to-all-done.1 = bf16[256,2,4096]{2,1,0:T(2,128)(2,1)} async-done(((bf16[256,2,4096]{2,1,0:T(2,128)(2,1)}), bf16[256,2,4096]{2,1,0:T(2,128)(2,1)}, u32[]{:S(2)}, u32[]{:S(2)}) %all-to-all-start.1) | async-done | bytes 4194336 | tf_op jit(solution)/shard_map/all_to_all | solution.py:95
  237.7 14.2 %reshape.79 = bf16[256,4,32,64]{3,2,1,0:T(8,128)(2,1)} reshape(bf16[256,2,4096]{2,1,0:T(2,128)(2,1)} %all-to-all-done.1) | data formatting | bytes 8388608
  256.9 61.6 %while.20 = (s32[]{:T(128)}, bf16[8,4,128,128]{3,2,1,0:T(8,128)(2,1)}, s32[8]{0:T(128)S(1)}, bf16[128,32,32]{0,2,1:T(8,128)(2,1)S(1)}, bf16[64,128,32]{1,0,2:T(8...) while((s32[]{:T(128)}, ...), condition=%wide.region_4.5_spmd, body=%wide.region_0.4_spmd.sunk | while | flops 270796800 | bytes 14824685 | solution.py:159
  318.5 45.8 %while.21 = (s32[]{:T(128)}, bf16[8,512,128]{2,1,0:T(8,128)(2,1)}, bf16[8,512,128]{2,1,0:T(8,128)(2,1)}, f32[128]{0:T(128)S(1)}, bf16[128,512]{1,0:T(8,128)(2,1)...) while((s32[]{:T(128)}, bf16[8,512,128]{2,1,0:T(8,128)(2,1)}, ...), condition=%wide.region_8.9_spmd, body=%wide.region_5.8_spmd.sunk | while | flops 204145152 | bytes 3301981 | solution.py:51
  322.0 2.3 fusion.89
  327.7 2.3 fusion.89
  333.4 2.3 fusion.89
  339.1 2.3 fusion.89
  344.8 2.3 fusion.89
  350.5 2.3 fusion.89
  356.3 2.3 fusion.89
  362.0 2.3 fusion.89
  364.3 20.7 %all_to_all.58 = bf16[32,128,128]{2,1,0:T(8,128)(2,1)S(1)} all-to-all(bf16[32,128,128]{2,1,0:T(8,128)(2,1)} %bitcast.140), channel_id=1, replica_groups=mesh['row'=32,'col'=8] {'col'}, dimensions={0} | all-to-all | bytes 2097152 | tf_op jit(solution)/shard_map/all_to_all | solution.py:60
  385.9 33.8 %all_to_all.59 = bf16[4,1024,128]{2,0,1:T(4,128)(2,1)S(1)} all-to-all(bf16[4,1024,128]{2,0,1:T(4,128)(2,1)S(1)} %copy.46), channel_id=1, replica_groups=mesh['row'=32,'col'=8] {'row'}, dimensions={1} | all-to-all | bytes 2097152 | tf_op jit(solution)/shard_map/all_to_all | solution.py:59
  420.1 19.8 %all_to_all.60 = bf16[8,4,4,32,128]{4,3,2,1,0:T(8,128)(2,1)S(1)} all-to-all(bf16[8,4,4,32,128]{4,3,2,1,0:T(8,128)(2,1)S(1)} %bitcast.145), channel_id=1, replica_groups=mesh['row'=32,'col'=8] {'col'}, dimensions={0} | all-to-all | bytes 2097152 | tf_op jit(solution)/shard_map/all_to_all | solution.py:67
  (172 shorter events, 95.6 us)
Async XLA Ops:
  0.6 439.8 %copy-start = (bf16[128,64]{0,1:T(8,128)(2,1)S(1)}, bf16[128,64]{0,1:T(8,128)(2,1)}, u32[]{:S(2)}) copy-start(bf16[128,64]{0,1:T(8,128)(2,1)} %param.28) | copy-start | bytes 49156
  20.9 111.9 %all-to-all-start = ((bf16[256,2,4096]{2,1,0:T(2,128)(2,1)}), bf16[256,2,4096]{2,1,0:T(2,128)(2,1)}, u32[]{:S(2)}, u32[]{:S(2)}) async-start(bf16[256,2,4096]{2,1,0:T(2,128)(2,1)} %reshape.76), calls=%async_computation | async-start | bytes 8388608 | tf_op jit(solution)/shard_map/all_to_all | solution.py:95
  55.9 87.2 %copy-start.3 = (bf16[128,4,32]{0,2,1:T(8,128)(2,1)S(1)}, bf16[128,4,32]{0,2,1:T(8,128)(2,1)}, u32[]{:S(2)}) copy-start(bf16[128,4,32]{0,2,1:T(8,128)(2,1)} %param.18) | copy-start | bytes 98308
  132.7 105.0 %all-to-all-start.1 = ((bf16[256,2,4096]{2,1,0:T(2,128)(2,1)}), bf16[256,2,4096]{2,1,0:T(2,128)(2,1)}, u32[]{:S(2)}, u32[]{:S(2)}) async-start(bf16[256,2,4096]{2,1,0:T(2,128)(2,1)} %reshape.78), calls=%async_computation.1 | async-start | bytes 8388608 | tf_op jit(solution)/shard_map/all_to_all | solution.py:95
  251.9 4.9 %copy-start.6 = (bf16[1024,128]{1,0:T(8,128)(2,1)S(1)}, bf16[1024,128]{1,0:T(8,128)(2,1)}, u32[]{:S(2)}) copy-start(bf16[1024,128]{1,0:T(8,128)(2,1)} %param.22) | copy-start | bytes 786436
  251.9 5.0 %copy-start.8 = (f32[128]{0:T(128)S(1)}, f32[128]{0:T(128)}, u32[]{:S(2)}) copy-start(f32[128]{0:T(128)} %param.23) | copy-start | bytes 1540
  256.9 61.6 %copy-start.2 = (bf16[128,512]{1,0:T(8,128)(2,1)S(1)}, bf16[128,512]{1,0:T(8,128)(2,1)}, u32[]{:S(2)}) copy-start(bf16[128,512]{1,0:T(8,128)(2,1)} %param.25) | copy-start | bytes 393220
  256.9 61.6 %copy-start.4 = (f32[128]{0:T(128)S(1)}, f32[128]{0:T(128)}, u32[]{:S(2)}) copy-start(f32[128]{0:T(128)} %param.24) | copy-start | bytes 1540
  256.9 61.6 %copy-start.7 = (bf16[128,512]{1,0:T(8,128)(2,1)S(1)}, bf16[128,512]{1,0:T(8,128)(2,1)}, u32[]{:S(2)}) copy-start(bf16[128,512]{1,0:T(8,128)(2,1)} %param.26) | copy-start | bytes 393220
  419.9 21.0 %copy-start.1 = (bf16[8,512,128]{2,1,0:T(8,128)(2,1)S(1)}, bf16[8,512,128]{2,1,0:T(8,128)(2,1)}, u32[]{:S(2)}) copy-start(bf16[8,512,128]{2,1,0:T(8,128)(2,1)} %get-tuple-element.101) | copy-start | bytes 3145732
  419.9 21.0 %copy-start.5 = (f32[64]{0:T(128)S(1)}, f32[64]{0:T(128)}, u32[]{:S(2)}) copy-start(f32[64]{0:T(128)} %param.29) | copy-start | bytes 772
